TPU v7x, 256 devices: a whole 4x4x8 slice. The times are simulated.
256 devices in a mesh: section: 4 (over y), expert: 64 (over z, x, core).
Axes of the slice: x: 4, y: 4, z: 8, core: 2. Of those that a mesh axis runs over, the one named last changes fastest.
Arguments:
- fresh: bfloat16 [8192, 2048], P('expert'), may hold values from -6 to 6
- previous: bfloat16 [4, 8192, 2048], P('section', 'expert'), may hold values from -6 to 6
- norm_gain: float32 [4, 2048], P('section'), may hold values from 0.1 to 1.9
- routes: int32 [4, 8192, 8], P('section', 'expert'), may hold values from 0 to 63, all different within a row; in each aligned block of 128 rows (0 to 127, 128 to 255, ..., all dimensions but the last counted through in order) at most 17 rows name the same one
- gate_weights: float32 [4, 8192, 8], P('section', 'expert'), may hold values from 0.03 to 0.3
- w_gate_up: bfloat16 [4, 64, 2048, 1536], P('section', 'expert'), may hold values from -0.125 to 0.125
- w_down: bfloat16 [4, 64, 768, 2048], P('section', 'expert'), may hold values from -0.21875 to 0.21875
Outputs:
- section_output: bfloat16 [4, 8192, 2048], P('section', 'expert')
Inputs may be any that keep to these rules, and one draw needn't show every extreme that they name: `routes`: within one section, among the 128 tokens of one device (aligned blocks of tokens) no expert is chosen by more than 17 tokens, and some expert is chosen by exactly 17 of them; the 8 experts of a token differ.
All inputs are finite; a program needn't handle non-finite values.
Results may differ from a plain program's by a relative error of at most 0.0033.
Values may be sent and summed in bfloat16 or wider, within the bound.
A program may use at most 64 MiB of HBM per device.

v0:
```python
import jax
import jax.numpy as jnp
from jax import lax
from jax.sharding import PartitionSpec as P

epsilon = 1e-06


def from_behind(value, axis, by):
    peers = lax.axis_size(axis)
    pairs = [(i, i + by) for i in range(peers) if 0 <= i + by < peers]
    return lax.ppermute(value, axis, pairs)


def body(fresh, previous, norm_gain, routes, gate_weights, w_gate_up, w_down):
    devices_exp = lax.axis_size("expert")
    section_id = lax.axis_index("section")
    tok_dev = fresh.shape[0]
    width = fresh.shape[1]
    topk_count = routes.shape[2]
    local_experts = w_gate_up.shape[1]
    hidden_units = w_down.shape[2]
    experts_total = devices_exp * local_experts
    capacity = min(tok_dev, 17 * tok_dev * topk_count // (16 * experts_total))
    total_rows = tok_dev * topk_count
    arrived = from_behind(previous[0], "section", 1)
    arrival = jnp.where(section_id == 0, fresh, arrived)
    wide_input = arrival.astype(jnp.float32)
    scale = lax.rsqrt(jnp.mean(wide_input * wide_input, axis=-1, keepdims=True) + epsilon)
    normed = (wide_input * scale * norm_gain[0][None, :]).astype(jnp.bfloat16)
    flat_ids = routes[0].reshape(-1)
    one_hot = (flat_ids[:, None] == jnp.arange(experts_total, dtype=jnp.int32)[None, :]).astype(
        jnp.int32
    )
    slot_rank = jnp.sum(jnp.cumsum(one_hot, axis=0) * one_hot, axis=1) - 1
    position = flat_ids * capacity + slot_rank
    source_row = (
        jnp.full((experts_total * capacity,), total_rows, jnp.int32)
        .at[position]
        .set(jnp.arange(total_rows, dtype=jnp.int32))
    )
    padded = jnp.concatenate([normed, jnp.zeros((1, width), jnp.bfloat16)], axis=0)
    send_buffer = padded[source_row // topk_count].reshape(
        devices_exp, local_experts, capacity, width
    )
    received = lax.all_to_all(send_buffer, "expert", split_axis=0, concat_axis=0, tiled=True)
    projected = jnp.einsum(
        "secd,edf->secf", received, w_gate_up[0], preferred_element_type=jnp.float32
    )
    hidden = (jax.nn.silu(projected[..., :hidden_units]) * projected[..., hidden_units:]).astype(
        jnp.bfloat16
    )
    returned = lax.all_to_all(
        jnp.einsum("secf,efd->secd", hidden, w_down[0], preferred_element_type=jnp.float32).astype(
            jnp.bfloat16
        ),
        "expert",
        split_axis=0,
        concat_axis=0,
        tiled=True,
    )
    flat_back = returned.reshape(experts_total * capacity, width)
    picked = flat_back[position].reshape(tok_dev, topk_count, width).astype(jnp.float32)
    mixed = jnp.sum(picked * gate_weights[0][:, :, None], axis=1)
    return (wide_input + mixed).astype(jnp.bfloat16)[None]


def solution(mesh):
    return jax.shard_map(
        body,
        mesh=mesh,
        in_specs=(
            P("expert", None),
            P("section", "expert", None),
            P("section", None),
            P("section", "expert", None),
            P("section", "expert", None),
            P("section", "expert", None, None),
            P("section", "expert", None, None),
        ),
        out_specs=P("section", "expert", None),
        check_vma=False,
    )
```

profile of v0, /device:TPU:32, one launch (start us, length us, event | category | flops | bytes accessed | tf_op | source)
XLA Modules:
  0.0 421.8 jit_solution(9765902958919063633)
XLA Ops:
  0.0 4.5 %collective-permute-start = (bf16[128,2048]{1,0:T(8,128)(2,1)}, bf16[128,2048]{1,0:T(8,128)(2,1)}, u32[]{:S(2)}, u32[]{:S(2)}) collective-permute-start(bf16[128,2048]{1,0:T(8,128)(2,1)} %bitcast.65), channel_id=1, source_target_pairs={{0,64},{64,128},{128,192},{1,65},{65,129},{129,193},{2,66},{66,130... | collective-permute-start | bytes 1572872 | tf_op jit(solution)/shard_map/ppermute | solution.py:12
  4.5 0.8 copy.18
  5.5 0.7 broadcast_multiply_fusion
  6.2 0.7 fusion.21
  6.9 31.1 %reduce-window.6 = s32[64,8,128]{2,1,0:T(8,128)S(1)} reduce-window(s32[64,8,128]{2,1,0:T(8,128)} %fusion.21, s32[]{:T(128)} %constant.21.clone.1), window={size=1x1x128 pad=0_0x0_0x127_0}, to_apply=%region_1.2 | reduce-window | flops 8323072 | bytes 524292 | tf_op jit(solution)/shard_map/reduce-window
  38.0 0.8 slice.20
  38.9 1.1 copy.20
  40.5 4.3 %scatter_custom_fusion = s32[1088]{0:T(1024)S(1)} fusion(s32[1024]{0:T(1024)S(1)} %bitcast.60, s32[1024]{0:T(1024)S(1)} %iota.11, s32[]{:T(128)} %constant.42.clone.1), kind=kCustom, calls=%fused_computation.41 | custom fusion | bytes 4356 | tf_op jit(solution)/shard_map/scatter | solution.py:40
  44.9 1.3 fusion.14
  46.2 0.8 copy-done.1
  47.0 0.2 fusion.16
  47.2 0.8 concatenate.3
  48.0 11.7 %gather_fusion = bf16[1088,2048]{1,0:T(8,128)(2,1)} fusion(bf16[129,2048]{1,0:T(8,128)(2,1)} %concatenate.3, s32[2048]{0:T(1024)S(1)} %pad_clamp_fusion), kind=kCustom, calls=%fused_computation | custom fusion | bytes 8917248 | tf_op jit(solution)/shard_map/gather | solution.py:43
  59.7 7.6 %reshape.86 = bf16[64,1,17,2048]{3,2,0,1:T(8,128)(2,1)} reshape(bf16[1088,2048]{1,0:T(8,128)(2,1)} %gather_fusion) | data formatting | bytes 8912896 | tf_op jit(solution)/shard_map/reshape | solution.py:43
  67.4 151.9 %all_to_all.10 = bf16[64,1,17,2048]{3,2,1,0:T(8,128)(2,1)S(1)} all-to-all(bf16[64,1,17,2048]{3,2,1,0:T(8,128)(2,1)} %bitcast.57), channel_id=1, replica_groups=mesh['section'=4,'expert'=64] {'expert'}, dimensions={0} | all-to-all | bytes 8912896 | tf_op jit(solution)/shard_map/all_to_all | solution.py:46
  219.2 19.1 %fusion.5 = f32[64,1,17,1536]{3,0,2,1:T(8,128)S(1)} fusion(bf16[1,1,2048,1536]{3,2,1,0:T(8,128)(2,1)} %param.12, bf16[64,1,17,2048]{3,2,1,0:T(8,128)(2,1)S(1)} %all_to_all.10), kind=kOutput, calls=%fused_computation.10 | convolution fusion | flops 6845104128 | bytes 17432576 | tf_op jit(solution)/shard_map/secd,edf->secf/dot_general | solution.py:47
  238.3 4.1 convert_bitcast_fusion
  242.5 5.3 %copy.24 = bf16[64,1,17,2048]{3,2,1,0:T(8,128)(2,1)} copy(bf16[64,1,17,2048]{3,0,2,1:T(8,128)(2,1)S(1)} %convert_bitcast_fusion) | data formatting | bytes 8912896 | tf_op jit(solution)/shard_map/convert_element_type | solution.py:54
  247.8 6.6 %all-to-all-start.1 = ((bf16[64,1,17,2048]{3,2,1,0:T(8,128)(2,1)}), bf16[64,1,17,2048]{3,2,1,0:T(8,128)(2,1)}, u32[]{:S(2)}, u32[]{:S(2)}) async-start(bf16[64,1,17,2048]{3,2,1,0:T(8,128)(2,1)} %copy.24), calls=%async_computation.1 | async-start | bytes 12582912 | tf_op jit(solution)/shard_map/all_to_all | solution.py:53
  254.5 140.3 %all-to-all-done.1 = bf16[64,1,17,2048]{3,2,1,0:T(8,128)(2,1)} async-done(((bf16[64,1,17,2048]{3,2,1,0:T(8,128)(2,1)}), bf16[64,1,17,2048]{3,2,1,0:T(8,128)(2,1)}, u32[]{:S(2)}, u32[]{:S(2)}) %all-to-all-start.1) | async-done | bytes 4456480 | tf_op jit(solution)/shard_map/all_to_all | solution.py:53
  394.9 7.8 %reshape.91 = bf16[1088,2048]{1,0:T(8,128)(2,1)} reshape(bf16[64,1,17,2048]{3,2,1,0:T(8,128)(2,1)} %all-to-all-done.1) | data formatting | bytes 8912896 | tf_op jit(solution)/shard_map/reshape | solution.py:62
  402.6 11.7 %gather_fusion.1 = bf16[1024,2048]{1,0:T(8,128)(2,1)} fusion(bf16[1088,2048]{1,0:T(8,128)(2,1)} %reshape.91, s32[1024]{0:T(1024)S(1)} %broadcast_clamp_fusion), kind=kCustom, calls=%fused_computation.1 | custom fusion | bytes 8392704 | tf_op jit(solution)/shard_map/gather | solution.py:63
  414.3 6.6 %fusion = f32[128,2048]{1,0:T(8,128)S(1)} fusion(bf16[1024,2048]{1,0:T(8,128)(2,1)} %gather_fusion.1, f32[128,8]{1,0:T(8,128)S(1)} %copy.25), kind=kLoop, calls=%fused_computation.4 | loop fusion | flops 6029312 | bytes 5246976 | tf_op jit(solution)/shard_map/reduce_sum | solution.py:64
  420.9 0.9 fusion.18
  (27 shorter events, 0.9 us)
Async XLA Ops:
  0.0 238.3 %copy-start = (bf16[1,1,768,2048]{3,2,1,0:T(8,128)(2,1)S(1)}, bf16[1,1,768,2048]{3,2,1,0:T(8,128)(2,1)}, u32[]{:S(2)}) copy-start(bf16[1,1,768,2048]{3,2,1,0:T(8,128)(2,1)} %param.13) | copy-start | bytes 9437188
  0.0 47.0 %copy-start.3 = (f32[1,2048]{1,0:T(1,128)S(1)}, f32[1,2048]{1,0:T(1,128)}, u32[]{:S(2)}) copy-start(f32[1,2048]{1,0:T(1,128)} %param.9) | copy-start | bytes 24580
  0.0 44.9 %collective-permute-start = (bf16[128,2048]{1,0:T(8,128)(2,1)}, bf16[128,2048]{1,0:T(8,128)(2,1)}, u32[]{:S(2)}, u32[]{:S(2)}) collective-permute-start(bf16[128,2048]{1,0:T(8,128)(2,1)} %bitcast.65), channel_id=1, source_target_pairs={{0,64},{64,128},{128,192},{1,65},{65,129},{129,193},{2,66},{66,130... | collective-permute-start | bytes 1572872 | tf_op jit(solution)/shard_map/ppermute | solution.py:12
  46.2 0.8 copy-start.1
  247.8 6.6 %copy-start.4 = (f32[1,128,8]{1,2,0:T(8,128)S(1)}, f32[1,128,8]{1,2,0:T(8,128)}, u32[]{:S(2)}) copy-start(f32[1,128,8]{1,2,0:T(8,128)} %param.11) | copy-start | bytes 12292
  247.8 147.1 %all-to-all-start.1 = ((bf16[64,1,17,2048]{3,2,1,0:T(8,128)(2,1)}), bf16[64,1,17,2048]{3,2,1,0:T(8,128)(2,1)}, u32[]{:S(2)}, u32[]{:S(2)}) async-start(bf16[64,1,17,2048]{3,2,1,0:T(8,128)(2,1)} %copy.24), calls=%async_computation.1 | async-start | bytes 12582912 | tf_op jit(solution)/shard_map/all_to_all | solution.py:53
  414.3 6.6 %copy-start.2 = (bf16[128,2048]{1,0:T(8,128)(2,1)S(1)}, bf16[128,2048]{1,0:T(8,128)(2,1)}, u32[]{:S(2)}) copy-start(bf16[128,2048]{1,0:T(8,128)(2,1)} %copy-done.1) | copy-start | bytes 1572868
where the time goes:
time: 425 us; the launch traced here: 422 us
  blocking collectives  152 us (36%)
  waiting for transfers between devices  140 us (33%)
  local copies, waits for them, and re-layouts  53.3 us (13%)
  other arithmetic  41.8 us (10%)
  matrix products  23.2 us (5%)
  starting transfers between devices  11.2 us (3%)
    all_to_all x1, blocking collectives, body(): lax.all_to_all(send_buffer, 'expert', split_axis=0, concat_axis=0, tiled=...  152 us
    all_to_all x1, waiting for transfers between devices, body(): lax.all_to_all(jnp.einsum('secf,efd->secd', hidden, w_down[0], preferred_...  140 us
    another operation x3, other arithmetic  31.3 us
    dot_general x1, matrix products, body(): jnp.einsum('secd,edf->secf', received, w_gate_up[0], preferred_element_ty...  19.1 us
    gather x1, local copies, waits for them, and re-layouts, body(): padded[source_row // topk_count]  11.7 us
    gather x1, local copies, waits for them, and re-layouts, body(): flat_back[position].reshape(tok_dev, topk_count, width).astype(jnp.float32)  11.7 us
  transfers between devices with their start and end apart: 2, of which 1 were waited for; matrix products, arithmetic and copies ran while one was open for 10% of the time, Pallas kernels for 0%

commit v1 on v0

v1 whole, which is shorter than its diff:
```python
import functools

import jax
import jax.numpy as jnp
from jax import lax
from jax.experimental import pallas as pl
from jax.experimental.pallas import tpu as pltpu
from jax.sharding import PartitionSpec as P

EPS = 1e-06
SLOT = 16
MESH = pl.DeviceIdType.MESH
F32, BF16 = jnp.float32, jnp.bfloat16


def kernel(
    Z, J, K,
    prev, fresh, gain, aux, wgu_h, wd_h, out,
    wgu, wd, fr, yr, arr, ag, auxb, x1s, x1r, yb, x2r, rss, rsr, hid, pf, sel8, ranks, gates,
    ysem, yrem, lsem, zss, zrs, axs, axr, x1ss, x1rs, x2ss, x2rs, rsss, rsrs,
):
    T, D = arr.shape
    HT = T // 2
    F = wd.shape[0]
    R = J * SLOT
    TN = min(512, D)
    TF = min(256, F)
    sec, nsec = lax.axis_index("section"), lax.axis_size("section")
    e = lax.axis_index("expert")
    z, j = lax.div(e, J), lax.rem(e, J)
    up = lax.rem(z + 1, Z) * J + j
    dn = lax.rem(z + Z - 1, Z) * J + j
    ynext, yprev = lax.rem(sec + 1, nsec), lax.rem(sec + nsec - 1, nsec)
    toward = (up, dn)
    half = (pl.ds(0, HT), pl.ds(HT, HT))
    order = [q for q in (4, 2, 6, 5, 3, 7, 1) if q < J]

    def remote(src, dst, ssem, rsem, expert):
        return pltpu.make_async_remote_copy(
            src_ref=src, dst_ref=dst, send_sem=ssem, recv_sem=rsem,
            device_id={"expert": expert}, device_id_type=MESH)

    loads = (
        pltpu.make_async_copy(fresh, fr, lsem.at[0]),
        pltpu.make_async_copy(wgu_h.at[0, 0], wgu, lsem.at[1]),
        pltpu.make_async_copy(wd_h.at[0, 0], wd, lsem.at[2]),
    )
    for c in loads:
        c.start()

    barrier = pltpu.get_barrier_semaphore()
    for t in (up, dn):
        pl.semaphore_signal(barrier, inc=1, device_id={"expert": t}, device_id_type=MESH)
    for q in order:
        pl.semaphore_signal(
            barrier, inc=1, device_id={"expert": z * J + lax.rem(j + q, J)}, device_id_type=MESH)
    for t in (ynext, yprev):
        pl.semaphore_signal(barrier, inc=1, device_id={"section": t}, device_id_type=MESH)
    pl.semaphore_wait(barrier, 4 + len(order))

    ycopies = [
        pltpu.make_async_remote_copy(
            src_ref=prev.at[0, half[h]], dst_ref=yr.at[half[h]], send_sem=ysem.at[h],
            recv_sem=yrem.at[h], device_id={"section": ynext}, device_id_type=MESH)
        for h in range(2)
    ]
    for c in ycopies:
        c.start()

    def zcopy(d, k, h, src):
        dst = 2 * k - 1 if d == 0 else jnp.minimum(2 * k, 7)
        return remote(ag.at[src, half[h]], ag.at[dst, half[h]], zss.at[d, k - 1, h],
                      zrs.at[d, k - 1, h], toward[d])

    def acopy(d, k, src):
        dst = 2 * k - 1 if d == 0 else jnp.minimum(2 * k, 7)
        return remote(auxb.at[src], auxb.at[dst], axs.at[d, k - 1], axr.at[d, k - 1], toward[d])

    auxb[0] = aux[...]
    acopy(0, 1, 0).start()
    acopy(1, 1, 0).start()
    loads[0].wait()
    for h in range(2):
        ycopies[h].wait_recv()
        x = jnp.where(sec == 0, fr[half[h], :].astype(F32), yr[half[h], :].astype(F32))
        arr[half[h], :] = x.astype(BF16)
        scale = lax.rsqrt(jnp.mean(x * x, axis=-1, keepdims=True) + EPS)
        ag[0, half[h], :] = (x * scale * gain[...]).astype(BF16)
        zcopy(0, 1, h, 0).start()
        zcopy(1, 1, h, 0).start()

    slot3 = lax.broadcasted_iota(jnp.int32, (J, SLOT, T), 1).astype(F32)
    first = (z * J).astype(F32)

    def own_rows(q):
        return pl.ds(pl.multiple_of(q * SLOT, SLOT), SLOT)

    def xcopy(src, dst, ssem, rsem, v, q):
        pj = lax.rem(j + q, J)
        return remote(src.at[v, own_rows(pj)], dst.at[v, own_rows(j)], ssem.at[v], rsem.at[v],
                      z * J + pj)

    def xwait(buf, sem, v):
        part = buf.at[v, pl.ds(0, R - SLOT)]
        pltpu.make_async_copy(part, part, sem.at[v]).wait()

    def xsend(src, dst, ssem, rsem, v):
        dst[v, own_rows(j), :] = src[v, own_rows(j), :]
        for q in order:
            xcopy(src, dst, ssem, rsem, v, q).start()

    def pick(matrix, source, v):
        def tile(n, _):
            c = pl.ds(pl.multiple_of(n * TN, TN), TN)
            x1s[v, :, c] = jnp.dot(matrix, source(c), preferred_element_type=F32).astype(BF16)
            return 0
        lax.fori_loop(0, D // TN, tile, 0)
        xsend(x1s, x1r, x1ss, x1rs, v)

    def select(u):
        a = auxb[u]
        expert = lax.broadcasted_iota(jnp.int32, (J, T), 0).astype(F32) + first
        mask, gate = jnp.zeros((J, T), F32), jnp.zeros((J, T), F32)
        for k in range(K):
            hit = a[k:k + 1, :] == expert
            mask = mask + jnp.where(hit, 1.0, 0.0)
            gate = gate + jnp.where(hit, a[8 + k:9 + k, :], 0.0)
        before = (lax.broadcasted_iota(jnp.int32, (T, T), 0)
                  < lax.broadcasted_iota(jnp.int32, (T, T), 1))
        tri = jnp.where(before, 1.0, 0.0).astype(BF16)
        rank = jnp.dot(mask.astype(BF16), tri, preferred_element_type=F32)
        rank = jnp.where(mask > 0.5, rank, -1.0)
        ranks[u] = rank
        gates[u] = gate
        r3 = jnp.broadcast_to(rank[:, None, :], (J, SLOT, T))
        uf = jnp.asarray(u, jnp.int32).astype(F32)
        sel = jnp.where(r3 == slot3, 1.0, 0.0).reshape(R, T).astype(BF16)
        extra = jnp.where(r3 == float(SLOT), 1.0, 0.0) * jnp.where(slot3 == uf, 1.0, 0.0)
        sel8[:, pl.ds(pl.multiple_of(u * T, T), T)] = extra.reshape(R, T).astype(BF16)
        pick(sel, lambda c: ag[u, :, c], u + 1)

    def ffn(v):
        def rise(n, _):
            lo = pl.ds(pl.multiple_of(n * TF, TF), TF)
            hi = pl.ds(pl.multiple_of(F + n * TF, TF), TF)
            x = x1r[pl.ds(v, 2)].reshape(2 * R, D)
            g = jnp.dot(x, wgu[:, lo], preferred_element_type=F32)
            w = jnp.dot(x, wgu[:, hi], preferred_element_type=F32)
            hid[:, lo] = (g / (1.0 + jnp.exp(-g)) * w).astype(BF16)
            return 0

        def fall(n, _):
            c = pl.ds(pl.multiple_of(n * TN, TN), TN)
            y = jnp.dot(hid[...], wd[:, c], preferred_element_type=F32)
            yb[pl.ds(v, 2), :, c] = y.astype(BF16).reshape(2, R, TN)
            return 0
        lax.fori_loop(0, F // TF, rise, 0)
        lax.fori_loop(0, D // TN, fall, 0)

    x1r[0] = jnp.zeros((R, D), BF16)
    select(0)
    loads[1].wait()
    loads[2].wait()

    def step(k, _):
        acopy(0, k, 0).wait_recv()
        acopy(1, k, 0).wait_recv()
        acopy(0, k + 1, 2 * k - 1).start()

        @pl.when(k < 3)
        def _():
            acopy(1, k + 1, 2 * k).start()
        for h in range(2):
            for d in range(2):
                zcopy(d, k, h, 0).wait_recv()
                forward = functools.partial(zcopy, d, k + 1, h, 2 * k - 1 + d)
                if d == h:
                    forward().start()
                else:
                    @pl.when(k < 3)
                    def _():
                        forward().start()
        select(2 * k - 1)
        select(2 * k)

        @pl.when(k > 1)
        def _():
            xwait(x1r, x1rs, 2 * k - 2)
        xwait(x1r, x1rs, 2 * k - 1)
        ffn(2 * k - 2)
        return 0
    lax.fori_loop(1, 4, step, 0)

    acopy(0, 4, 0).wait_recv()
    zcopy(0, 4, 0, 0).wait_recv()
    zcopy(1, 4, 1, 0).wait_recv()
    select(7)
    pick(sel8[...], lambda c: ag[:, :, c].reshape(8 * T, TN), 9)
    give = functools.partial(xsend, yb, x2r, x2ss, x2rs)
    give(1)

    def tail(g, _):
        xwait(x1r, x1rs, 2 * g - 2)
        xwait(x1r, x1rs, 2 * g - 1)
        ffn(2 * g - 2)
        return 0
    lax.fori_loop(4, 6, tail, 0)
    for u in (7, 8, 5, 6, 3, 4, 1, 2):
        give(u + 1)

    def combine(u, p):
        xwait(x2r, x2rs, u + 1)
        r3 = jnp.broadcast_to(ranks[u][:, None, :], (J, SLOT, T))
        g3 = jnp.broadcast_to(gates[u][:, None, :], (J, SLOT, T))
        c0 = jnp.where(r3 == slot3, g3, 0.0).reshape(R, T).T
        c8 = (jnp.where(r3 == float(SLOT), g3, 0.0)
              * jnp.where(slot3 == float(u), 1.0, 0.0)).reshape(R, T).T
        hi0, hi8 = c0.astype(BF16), c8.astype(BF16)
        lo0, lo8 = (c0 - hi0.astype(F32)).astype(BF16), (c8 - hi8.astype(F32)).astype(BF16)

        def tile(n, _):
            c = pl.ds(pl.multiple_of(n * TN, TN), TN)
            main, extra = x2r[u + 1, :, c], x2r[9, :, c]
            total = jnp.dot(hi0, main, preferred_element_type=F32)
            total += jnp.dot(lo0, main, preferred_element_type=F32)
            total += jnp.dot(hi8, extra, preferred_element_type=F32)
            total += jnp.dot(lo8, extra, preferred_element_type=F32)
            pf[p, :, c] = total
            return 0
        lax.fori_loop(0, D // TN, tile, 0)

    def rcopy(u, h, target):
        return remote(rss.at[u, half[h]], rsr.at[u, half[h]], rsss.at[u, h], rsrs.at[u, h], target)

    def pass_on(u, p, h, source, target):
        total = pf[p, half[h], :]
        if source is not None:
            rcopy(source, h, target).wait_recv()
            total = total + rsr[source, half[h], :].astype(F32)
        rss[u, half[h], :] = total.astype(BF16)
        rcopy(u, h, target).start()

    xwait(x2r, x2rs, 9)
    combine(7, 0)
    pass_on(7, 0, 0, None, dn)
    pass_on(7, 0, 1, None, up)
    combine(5, 0)
    pass_on(5, 0, 1, None, dn)
    combine(6, 1)
    pass_on(6, 1, 0, None, up)
    pass_on(5, 0, 0, 7, dn)
    pass_on(6, 1, 1, 7, up)
    for u in (3, 1):
        combine(u, 0)
        combine(u + 1, 1)
        for h in (1, 0):
            pass_on(u, 0, h, u + 2, dn)
            pass_on(u + 1, 1, 1 - h, u + 3, up)
    combine(0, 0)
    for h in range(2):
        rcopy(1, h, dn).wait_recv()
        rcopy(2, h, dn).wait_recv()
        total = (pf[0, half[h], :] + rsr[1, half[h], :].astype(F32)
                 + rsr[2, half[h], :].astype(F32))
        out[0, half[h], :] = (arr[half[h], :].astype(F32) + total).astype(BF16)

    for c in ycopies:
        c.wait_send()
    for k in range(1, 5):
        for d in range(2):
            if k < 4 or d == 0:
                acopy(d, k, 0).wait_send()
            for h in range(2):
                if k < 4 or d == h:
                    zcopy(d, k, h, 0).wait_send()
    for u in range(9):
        xwait(x1s, x1ss, u + 1)
        xwait(yb, x2ss, u + 1)
    for u in range(1, 8):
        for h in range(2):
            rcopy(u, h, dn).wait_send()


def body(J, fresh, previous, norm_gain, routes, gate_weights, w_gate_up, w_down):
    T, D = fresh.shape
    F = w_down.shape[2]
    K = routes.shape[2]
    Z = lax.axis_size("expert") // J
    R = J * SLOT
    pad = jnp.zeros((8 - K, T), F32)
    aux = jnp.concatenate(
        [routes[0].T.astype(F32), pad - 1.0, gate_weights[0].T, pad], axis=0)
    anywhere, vmem = pl.BlockSpec(memory_space=pl.ANY), pl.BlockSpec(memory_space=pltpu.VMEM)
    dma = pltpu.SemaphoreType.DMA
    return pl.pallas_call(
        functools.partial(kernel, Z, J, K),
        out_shape=jax.ShapeDtypeStruct((1, T, D), BF16),
        in_specs=[anywhere, anywhere, vmem, vmem, anywhere, anywhere],
        out_specs=vmem,
        scratch_shapes=[
            pltpu.VMEM((D, 2 * F), BF16), pltpu.VMEM((F, D), BF16),
            pltpu.VMEM((T, D), BF16), pltpu.VMEM((T, D), BF16), pltpu.VMEM((T, D), BF16),
            pltpu.VMEM((8, T, D), BF16), pltpu.VMEM((8, 16, T), F32),
            pltpu.VMEM((10, R, D), BF16), pltpu.VMEM((10, R, D), BF16),
            pltpu.VMEM((10, R, D), BF16), pltpu.VMEM((10, R, D), BF16),
            pltpu.VMEM((8, T, D), BF16), pltpu.VMEM((8, T, D), BF16),
            pltpu.VMEM((2 * R, F), BF16), pltpu.VMEM((2, T, D), F32),
            pltpu.VMEM((R, 8 * T), BF16), pltpu.VMEM((8, J, T), F32), pltpu.VMEM((8, J, T), F32),
            dma((2,)), dma((2,)), dma((3,)), dma((2, 4, 2)), dma((2, 4, 2)), dma((2, 4)),
            dma((2, 4)), dma((10,)), dma((10,)), dma((10,)), dma((10,)), dma((8, 2)), dma((8, 2)),
        ],
        compiler_params=pltpu.CompilerParams(
            collective_id=0, has_side_effects=True, vmem_limit_bytes=62 * 2**20),
    )(previous, fresh, norm_gain, aux, w_gate_up, w_down)


def solution(mesh):
    blocks = 8
    return jax.shard_map(
        functools.partial(body, mesh.shape["expert"] // blocks),
        mesh=mesh,
        in_specs=(
            P("expert", None),
            P("section", "expert", None),
            P("section", None),
            P("section", "expert", None),
            P("section", "expert", None),
            P("section", "expert", None, None),
            P("section", "expert", None, None),
        ),
        out_specs=P("section", "expert", None),
        check_vma=False,
    )
```

time: 425 us -> 151 us (0.36)
  blocking collectives: 152 us -> 0 us
  Pallas kernels: 0 us -> 146 us
  waiting for transfers between devices: 140 us -> 0 us
  local copies, waits for them, and re-layouts: 53.3 us -> 1.88 us
  other arithmetic: 41.8 us -> 1.97 us
  matrix products: 23.2 us -> 0 us
  starting transfers between devices: 11.2 us -> 0 us
    all_to_all x1 -> x0, blocking collectives: 152 us -> none  [body(): lax.all_to_all(send_buffer, 'expert', split_axis=0, concat_axis=0, tiled=...]
    pallas_call x0 -> x1, Pallas kernels: none -> 146 us  [body(): pl.pallas_call(functools.partial(kernel, Z, J, K), out_shape=jax.ShapeDty...]
    all_to_all x1 -> x0, waiting for transfers between devices: 140 us -> none  [body(): lax.all_to_all(jnp.einsum('secf,efd->secd', hidden, w_down[0], preferred_...]
    another operation x3 -> x0, other arithmetic: 31.3 us -> none
    gather x2 -> x0, local copies, waits for them, and re-layouts: 23.4 us -> none  [the longest x1 11.7 us: body(): padded[source_row // topk_count]]
    dot_general x2 -> x0, matrix products: 23.2 us -> none  [the longest x1 19.1 us: body(): jnp.einsum('secd,edf->secf', received, w_gate_up[0], preferred_element_ty...]
    reshape x2 -> x0, local copies, waits for them, and re-layouts: 15.4 us -> none  [the longest x1 7.77 us: body(): flat_back = returned.reshape(experts_total * capacity, width)]
    reduce_sum x3 -> x0, other arithmetic: 7.95 us -> none  [the longest x1 6.57 us: body(): mixed = jnp.sum(picked * gate_weights[0][:, :, None], axis=1)]
  transfers between devices with their start and end apart: 2 -> 0, of which waited for: 1 -> 0; matrix products, arithmetic and copies ran while one was open for 10% -> 0% of each run, Pallas kernels for 0% -> 0%
where the time goes in v1:
time: 151 us; the launch traced here: 150 us
  Pallas kernels  146 us (97%)
  other arithmetic  1.97 us (1%)
  local copies, waits for them, and re-layouts  1.88 us (1%)
    pallas_call x1, Pallas kernels, body(): pl.pallas_call(functools.partial(kernel, Z, J, K), out_shape=jax.ShapeDty...  146 us

profile of v1, /device:TPU:32, one launch (start us, length us, event | category | flops | bytes accessed | tf_op | source)
XLA Modules:
  0.0 149.8 jit_solution(16792512943173470146)
XLA Ops:
  0.0 0.7 convert_bitcast_fusion
  0.7 1.3 pad_maximum_fusion.aux
  2.0 145.9 %shard_map.73 = bf16[1,128,2048]{2,1,0:T(8,128)(2,1)} custom-call(bf16[1,128,2048]{2,1,0:T(8,128)(2,1)} %prev.1, bf16[128,2048]{1,0:T(8,128)(2,1)} %fresh.1, f32[1,2048]{1,0:T(1,128)} %gain.1, f32[16,128]{1,0:T(8,128)} %pad_maximum_fusion.aux, bf16[1,1,2048,1536]{3,2,1,0:T(8,128)(2,1)} %wgu_h.1, bf16[1,1,768,2048]{3,2,1,0:T(8,128)(2,1)} %wd_h.1), custom_call_target="tpu_custom_call" | custom-call | tf_op jit(solution)/shard_map/pallas_call | solution.py:295
  147.9 1.9 %copy.9 = bf16[1,128,2048]{2,1,0:T(8,128)(2,1)} copy(bf16[1,128,2048]{2,1,0:T(8,128)(2,1)} %shard_map.73) | data formatting | bytes 1048576

commit v2 on v1

v2 whole, which is shorter than its diff:
```python
import functools

import jax
import jax.numpy as jnp
from jax import lax
from jax.experimental import pallas as pl
from jax.experimental.pallas import tpu as pltpu
from jax.sharding import PartitionSpec as P

EPS = 1e-06
SLOT = 16
PIECES = 4
RETURNS = (
    (7, 0), (8, 0), (3, 0), (4, 0), (1, 0), (2, 0), (7, 1), (8, 1), (5, 1), (6, 1), (3, 1), (4, 1),
    (1, 1), (2, 1), (0, 0), (0, 1),
)
MESH = pl.DeviceIdType.MESH
F32, BF16 = jnp.float32, jnp.bfloat16


def kernel(
    Z, J,
    prev, fresh, gain, routes, weights, wgu_h, wd_h, out,
    wgu, wd, fr, yr, arr, ag, auxb, x1s, x1r, x1e, x1f, yb, ye, x2r, x2e, rss, rsr, hid, pf,
    sel8, ranks, gates,
    ysem, yrem, lsem, zss, zrs, axs, axr, x1ss, x1rs, x2ss, x2rs, rsss, rsrs,
):
    T, D = arr.shape
    K = routes.shape[0]
    F = wd.shape[0]
    R = J * SLOT
    CW, TN, TF = D // 2, D // 4, min(256, F)
    sec, nsec = lax.axis_index("section"), lax.axis_size("section")
    e = lax.axis_index("expert")
    z, j = lax.div(e, J), lax.rem(e, J)
    up = lax.rem(z + 1, Z) * J + j
    dn = lax.rem(z + Z - 1, Z) * J + j
    ynext, yprev = lax.rem(sec + 1, nsec), lax.rem(sec + nsec - 1, nsec)
    toward = (up, dn)
    piece = [pl.ds(p * (T // PIECES), T // PIECES) for p in range(PIECES)]
    order = [q for q in (4, 2, 6, 5, 3, 7, 1) if q < J]

    def remote(src, dst, ssem, rsem, expert):
        return pltpu.make_async_remote_copy(
            src_ref=src, dst_ref=dst, send_sem=ssem, recv_sem=rsem,
            device_id={"expert": expert}, device_id_type=MESH)

    def columns(n, width):
        return pl.ds(pl.multiple_of(n * width, width), width)

    barrier = pltpu.get_barrier_semaphore()
    for t in (ynext, yprev):
        pl.semaphore_signal(barrier, inc=1, device_id={"section": t}, device_id_type=MESH)
    for t in (up, dn):
        pl.semaphore_signal(barrier, inc=1, device_id={"expert": t}, device_id_type=MESH)
    for q in order:
        pl.semaphore_signal(
            barrier, inc=1, device_id={"expert": z * J + lax.rem(j + q, J)}, device_id_type=MESH)

    loads = (
        pltpu.make_async_copy(fresh, fr, lsem.at[0]),
        pltpu.make_async_copy(wgu_h.at[0, 0], wgu, lsem.at[1]),
        pltpu.make_async_copy(wd_h.at[0, 0], wd, lsem.at[2]),
    )
    loads[0].start()
    auxb[0] = jnp.full((16, T), -1.0, F32)
    auxb[0, 0:K, :] = routes[...].astype(F32)
    auxb[0, 8:8 + K, :] = weights[...]
    pl.semaphore_wait(barrier, 4 + len(order))

    ycopies = [
        pltpu.make_async_remote_copy(
            src_ref=prev.at[0, piece[p]], dst_ref=yr.at[piece[p]], send_sem=ysem.at[p],
            recv_sem=yrem.at[p], device_id={"section": ynext}, device_id_type=MESH)
        for p in range(PIECES)
    ]
    for c in ycopies:
        c.start()

    def zcopy(d, k, p, src):
        dst = 2 * k - 1 if d == 0 else jnp.minimum(2 * k, 7)
        return remote(ag.at[src, piece[p]], ag.at[dst, piece[p]], zss.at[d, k - 1, p],
                      zrs.at[d, k - 1, p], toward[d])

    def acopy(d, k, src):
        dst = 2 * k - 1 if d == 0 else jnp.minimum(2 * k, 7)
        return remote(auxb.at[src], auxb.at[dst], axs.at[d, k - 1], axr.at[d, k - 1], toward[d])

    def last_hop(d, p):
        return (p < PIECES // 2) == (d == 0)

    acopy(0, 1, 0).start()
    acopy(1, 1, 0).start()
    loads[1].start()
    loads[2].start()
    loads[0].wait()
    for p in range(PIECES):
        ycopies[p].wait_recv()
        x = jnp.where(sec == 0, fr[piece[p], :].astype(F32), yr[piece[p], :].astype(F32))
        arr[piece[p], :] = x.astype(BF16)
        scale = lax.rsqrt(jnp.mean(x * x, axis=-1, keepdims=True) + EPS)
        ag[0, piece[p], :] = (x * scale * gain[...]).astype(BF16)
        zcopy(0, 1, p, 0).start()
        zcopy(1, 1, p, 0).start()

    slot3 = lax.broadcasted_iota(jnp.int32, (J, SLOT, T), 1).astype(F32)
    slot3h = jnp.where(slot3 >= 8.0, slot3 - 8.0, slot3)
    first = (z * J).astype(F32)

    def own_rows(q):
        return pl.ds(pl.multiple_of(q * SLOT, SLOT), SLOT)

    def xwait(buf, cols, sem):
        part = buf.at[pl.ds(0, R - SLOT), cols]
        pltpu.make_async_copy(part, part, sem).wait()

    def exchange(src, dst, cols, ssem, rsem):
        dst[own_rows(j), cols] = src[own_rows(j), cols]
        for q in order:
            pj = lax.rem(j + q, J)
            remote(src.at[own_rows(pj), cols], dst.at[own_rows(j), cols], ssem, rsem,
                   z * J + pj).start()

    full, packed = pl.ds(0, D), pl.ds(0, CW)

    def select(u):
        a = auxb[u]
        expert = lax.broadcasted_iota(jnp.int32, (J, T), 0).astype(F32) + first
        mask, gate = jnp.zeros((J, T), F32), jnp.zeros((J, T), F32)
        for k in range(K):
            hit = a[k:k + 1, :] == expert
            mask = mask + jnp.where(hit, 1.0, 0.0)
            gate = gate + jnp.where(hit, a[8 + k:9 + k, :], 0.0)
        before = (lax.broadcasted_iota(jnp.int32, (T, T), 0)
                  < lax.broadcasted_iota(jnp.int32, (T, T), 1))
        tri = jnp.where(before, 1.0, 0.0).astype(BF16)
        rank = jnp.dot(mask.astype(BF16), tri, preferred_element_type=F32)
        rank = jnp.where(mask > 0.5, rank, -1.0)
        ranks[u] = rank
        gates[u] = gate
        r3 = jnp.broadcast_to(rank[:, None, :], (J, SLOT, T))
        uf = jnp.asarray(u, jnp.int32).astype(F32)
        sel = jnp.where(r3 == slot3, 1.0, 0.0).reshape(R, T).astype(BF16)
        extra = jnp.where(r3 == float(SLOT), 1.0, 0.0) * jnp.where(slot3h == uf, 1.0, 0.0)
        sel8[:, columns(u, T)] = extra.reshape(R, T).astype(BF16)

        def tile(n, _):
            c = columns(n, TN)
            x1s[u, :, c] = jnp.dot(sel, ag[u, :, c], preferred_element_type=F32).astype(BF16)
            return 0
        lax.fori_loop(0, D // TN, tile, 0)
        exchange(x1s.at[u], x1r.at[u + 1], full, x1ss.at[u], x1rs.at[u])

    low = lax.rem(lax.broadcasted_iota(jnp.int32, (R, TN), 0), SLOT) < 8

    def mover(shift, upper):
        r = lax.broadcasted_iota(jnp.int32, (R, R), 0)
        c = lax.broadcasted_iota(jnp.int32, (R, R), 1)
        wanted = (lax.rem(r, SLOT) >= 8) if upper else (lax.rem(r, SLOT) < 8)
        return jnp.where(wanted, jnp.where(c == r + shift, 1.0, 0.0), 0.0).astype(BF16)

    def select_extra():
        def tile(h, _):
            a = jnp.dot(sel8[...], ag[:, :, columns(2 * h, TN)].reshape(8 * T, TN),
                        preferred_element_type=F32)
            b = jnp.dot(sel8[...], ag[:, :, columns(2 * h + 1, TN)].reshape(8 * T, TN),
                        preferred_element_type=F32)
            x1e[:, columns(h, TN)] = jnp.where(low, a, b).astype(BF16)
            return 0
        lax.fori_loop(0, 2, tile, 0)
        exchange(x1e, x1f, packed, x1ss.at[8], x1rs.at[8])

    def spread_extra():
        down = mover(8, False)

        def tile(h, _):
            a = x1f[:, columns(h, TN)]
            x1r[9, :, columns(2 * h, TN)] = a
            x1r[9, :, columns(2 * h + 1, TN)] = jnp.dot(
                down, a, preferred_element_type=F32).astype(BF16)
            return 0
        lax.fori_loop(0, 2, tile, 0)

    def pack_extra():
        raised = mover(-8, True)

        def tile(h, _):
            a = yb[9, :, columns(2 * h, TN)].astype(F32)
            b = jnp.dot(raised, yb[9, :, columns(2 * h + 1, TN)], preferred_element_type=F32)
            ye[:, columns(h, TN)] = jnp.where(low, a, b).astype(BF16)
            return 0
        lax.fori_loop(0, 2, tile, 0)

    def ffn(v):
        def rise(n, _):
            lo = columns(n, TF)
            hi = pl.ds(pl.multiple_of(F + n * TF, TF), TF)
            x = x1r[pl.ds(v, 2)].reshape(2 * R, D)
            g = jnp.dot(x, wgu[:, lo], preferred_element_type=F32)
            w = jnp.dot(x, wgu[:, hi], preferred_element_type=F32)
            hid[:, lo] = (g / (1.0 + jnp.exp(-g)) * w).astype(BF16)
            return 0

        def fall(n, _):
            c = columns(n, TN)
            y = jnp.dot(hid[...], wd[:, c], preferred_element_type=F32)
            yb[pl.ds(v, 2), :, c] = y.astype(BF16).reshape(2, R, TN)
            return 0
        lax.fori_loop(0, F // TF, rise, 0)
        lax.fori_loop(0, D // TN, fall, 0)

    x1r[0] = jnp.zeros((R, D), BF16)
    select(0)
    loads[1].wait()
    loads[2].wait()

    def step(k, _):
        acopy(0, k, 0).wait_recv()
        acopy(1, k, 0).wait_recv()
        acopy(0, k + 1, 2 * k - 1).start()

        @pl.when(k < 3)
        def _():
            acopy(1, k + 1, 2 * k).start()
        for p in range(PIECES):
            for d in range(2):
                zcopy(d, k, p, 0).wait_recv()
                forward = functools.partial(zcopy, d, k + 1, p, 2 * k - 1 + d)
                if last_hop(d, p):
                    forward().start()
                else:
                    @pl.when(k < 3)
                    def _():
                        forward().start()
        select(2 * k - 1)
        select(2 * k)

        @pl.when(k > 1)
        def _():
            xwait(x1r.at[2 * k - 2], full, x1rs.at[2 * k - 3])
        xwait(x1r.at[2 * k - 1], full, x1rs.at[2 * k - 2])
        ffn(2 * k - 2)
        return 0
    lax.fori_loop(1, 4, step, 0)

    acopy(0, 4, 0).wait_recv()
    for p in range(PIECES):
        zcopy(0 if last_hop(0, p) else 1, 4, p, 0).wait_recv()
    select(7)
    select_extra()

    def give(u, h):
        if u < 8:
            exchange(yb.at[u + 1], x2r.at[u], columns(h, CW), x2ss.at[u, h], x2rs.at[u, h])
        else:
            exchange(ye, x2e, columns(h, TN), x2ss.at[u, h], x2rs.at[u, h])

    def tail(g, _):
        xwait(x1r.at[2 * g - 2], full, x1rs.at[2 * g - 3])

        @pl.when(g == 4)
        def _():
            xwait(x1r.at[7], full, x1rs.at[6])

        @pl.when(g == 5)
        def _():
            xwait(x1f, packed, x1rs.at[8])
            spread_extra()
        ffn(2 * g - 2)

        @pl.when(g == 4)
        def _():
            give(5, 0)
            give(6, 0)
        return 0
    lax.fori_loop(4, 6, tail, 0)
    pack_extra()
    for u, h in RETURNS:
        give(u, h)

    def combine(u, p, h):
        xwait(x2r.at[u], columns(h, CW), x2rs.at[u, h])
        r3 = jnp.broadcast_to(ranks[u][:, None, :], (J, SLOT, T))
        g3 = jnp.broadcast_to(gates[u][:, None, :], (J, SLOT, T))
        over = jnp.where(r3 == float(SLOT), g3, 0.0)
        parts = [jnp.where(r3 == slot3, g3, 0.0)]
        parts += [jnp.where(slot3 == float(u + 8 * i), over, 0.0) for i in range(2)]
        parts = [c.reshape(R, T).T for c in parts]
        high = [c.astype(BF16) for c in parts]
        rest = [(c - b.astype(F32)).astype(BF16) for c, b in zip(parts, high)]
        extra = x2e[:, columns(h, TN)]
        for i in range(2):
            main = x2r[u, :, columns(2 * h + i, TN)]
            total = jnp.dot(high[0], main, preferred_element_type=F32)
            total += jnp.dot(rest[0], main, preferred_element_type=F32)
            total += jnp.dot(high[1 + i], extra, preferred_element_type=F32)
            total += jnp.dot(rest[1 + i], extra, preferred_element_type=F32)
            pf[p, :, pl.ds(i * TN, TN)] = total

    def rcopy(u, h, target):
        return remote(rss.at[u, h], rsr.at[u, h], rsss.at[u, h], rsrs.at[u, h], target)

    def take(source, p, h, target):
        rcopy(source, h, target).wait_recv()
        pf[p] = pf[p] + rsr[source, h].astype(F32)

    def send_on(u, p, h, target):
        rss[u, h] = pf[p].astype(BF16)
        rcopy(u, h, target).start()

    def reduce_half(h, _):
        xwait(x2e, columns(h, TN), x2rs.at[8, h])
        combine(7, 0, h)
        send_on(7, 0, h, jnp.where(h == 0, dn, up))
        combine(5, 0, h)
        combine(6, 1, h)

        @pl.when(h == 0)
        def _():
            send_on(6, 1, h, up)
            take(7, 0, h, dn)
            send_on(5, 0, h, dn)

        @pl.when(h == 1)
        def _():
            send_on(5, 0, h, dn)
            take(7, 1, h, up)
            send_on(6, 1, h, up)
        for u in (3, 1):
            combine(u, 0, h)
            combine(u + 1, 1, h)
            take(u + 2, 0, h, dn)
            send_on(u, 0, h, dn)
            take(u + 3, 1, h, up)
            send_on(u + 1, 1, h, up)
        return 0
    lax.fori_loop(0, 2, reduce_half, 0)

    def finish(h, _):
        c = columns(h, CW)
        combine(0, 0, h)
        take(1, 0, h, dn)
        take(2, 0, h, up)
        out[0, :, c] = (arr[:, c].astype(F32) + pf[0]).astype(BF16)
        return 0
    lax.fori_loop(0, 2, finish, 0)

    for c in ycopies:
        c.wait_send()
    for k in range(1, 5):
        for d in range(2):
            if k < 4 or d == 0:
                acopy(d, k, 0).wait_send()
            for p in range(PIECES):
                if k < 4 or last_hop(d, p):
                    zcopy(d, k, p, 0).wait_send()
    for u in range(8):
        xwait(x1s.at[u], full, x1ss.at[u])
    xwait(x1e, packed, x1ss.at[8])
    for h in range(2):
        for u in range(8):
            xwait(x2r.at[u], columns(h, CW), x2ss.at[u, h])
        xwait(ye, columns(h, TN), x2ss.at[8, h])
        for u in range(1, 8):
            rcopy(u, h, dn).wait_send()


def body(J, fresh, previous, norm_gain, routes, gate_weights, w_gate_up, w_down):
    T, D = fresh.shape
    F = w_down.shape[2]
    Z = lax.axis_size("expert") // J
    R = J * SLOT
    anywhere, vmem = pl.BlockSpec(memory_space=pl.ANY), pl.BlockSpec(memory_space=pltpu.VMEM)
    dma = pltpu.SemaphoreType.DMA
    return pl.pallas_call(
        functools.partial(kernel, Z, J),
        out_shape=jax.ShapeDtypeStruct((1, T, D), BF16),
        in_specs=[anywhere, anywhere, vmem, vmem, vmem, anywhere, anywhere],
        out_specs=vmem,
        scratch_shapes=[
            pltpu.VMEM((D, 2 * F), BF16), pltpu.VMEM((F, D), BF16),
            pltpu.VMEM((T, D), BF16), pltpu.VMEM((T, D), BF16), pltpu.VMEM((T, D), BF16),
            pltpu.VMEM((8, T, D), BF16), pltpu.VMEM((8, 16, T), F32),
            pltpu.VMEM((8, R, D), BF16), pltpu.VMEM((10, R, D), BF16),
            pltpu.VMEM((R, D // 2), BF16), pltpu.VMEM((R, D // 2), BF16),
            pltpu.VMEM((10, R, D), BF16), pltpu.VMEM((R, D // 2), BF16),
            pltpu.VMEM((8, R, D), BF16), pltpu.VMEM((R, D // 2), BF16),
            pltpu.VMEM((8, 2, T, D // 2), BF16), pltpu.VMEM((8, 2, T, D // 2), BF16),
            pltpu.VMEM((2 * R, F), BF16), pltpu.VMEM((2, T, D // 2), F32),
            pltpu.VMEM((R, 8 * T), BF16), pltpu.VMEM((8, J, T), F32), pltpu.VMEM((8, J, T), F32),
            dma((PIECES,)), dma((PIECES,)), dma((3,)), dma((2, 4, PIECES)), dma((2, 4, PIECES)),
            dma((2, 4)), dma((2, 4)), dma((9,)), dma((9,)), dma((9, 2)), dma((9, 2)),
            dma((8, 2)), dma((8, 2)),
        ],
        compiler_params=pltpu.CompilerParams(
            collective_id=0, has_side_effects=True, vmem_limit_bytes=62 * 2**20),
    )(previous, fresh, norm_gain, routes[0].T, gate_weights[0].T, w_gate_up, w_down)


def solution(mesh):
    blocks = 8
    return jax.shard_map(
        functools.partial(body, mesh.shape["expert"] // blocks),
        mesh=mesh,
        in_specs=(
            P("expert", None),
            P("section", "expert", None),
            P("section", None),
            P("section", "expert", None),
            P("section", "expert", None),
            P("section", "expert", None, None),
            P("section", "expert", None, None),
        ),
        out_specs=P("section", "expert", None),
        check_vma=False,
    )
```

time: 151 us -> 145 us (0.960)
  Pallas kernels: 146 us -> 143 us
  other arithmetic: 1.97 us -> 0 us
    pallas_call x1, Pallas kernels: 146 us -> 143 us  [body(): pl.pallas_call(functools.partial(kernel, Z, J), out_shape=jax.ShapeDtypeS...]
where the time goes in v2:
time: 145 us
  Pallas kernels  143 us (99%)
  local copies, waits for them, and re-layouts  1.88 us (1%)
    pallas_call x1, Pallas kernels, body(): pl.pallas_call(functools.partial(kernel, Z, J), out_shape=jax.ShapeDtypeS...  143 us

profile of v2, /device:TPU:32, one launch (start us, length us, event | category | flops | bytes accessed | tf_op | source)
XLA Modules:
  0.0 145.1 jit_solution(15646966136906129410)
XLA Ops:
  0.0 143.2 %shard_map.73 = bf16[1,128,2048]{2,1,0:T(8,128)(2,1)} custom-call(bf16[1,128,2048]{2,1,0:T(8,128)(2,1)} %prev.1, bf16[128,2048]{1,0:T(8,128)(2,1)} %fresh.1, f32[1,2048]{1,0:T(1,128)} %gain.1, s32[8,128]{1,0:T(8,128)} %bitcast.6, f32[8,128]{1,0:T(8,128)} %bitcast.7, bf16[1,1,2048,1536]{3,2,1,0:T(8,128)(2,1)} %wgu_h.1, bf16[1,1,768,2048]{3,2,1,0:T(8,128)(2,1)} %wd_h.1), custom_call_target="tpu_custom_call" | custom-call | tf_op jit(solution)/shard_map/pallas_call | solution.py:375
  143.2 1.9 %copy.9 = bf16[1,128,2048]{2,1,0:T(8,128)(2,1)} copy(bf16[1,128,2048]{2,1,0:T(8,128)(2,1)} %shard_map.73) | data formatting | bytes 1048576
